TPU v7x, 256 devices: a whole 4x4x8 slice. The times are simulated.
256 devices in a mesh: alpha: 8 (over z_lo, y), beta: 32 (over z_hi, x, core).
Axes of the slice: x: 4, y: 4, z: 8 (z_hi: 4, z_lo: 2; z = z_hi * 2 + z_lo), core: 2. Of those that a mesh axis runs over, the one named last changes fastest.
Arguments:
- ci_vectors: bfloat16 [8, 4096, 4096], P(None, 'alpha', 'beta'), may hold values from -6 to 6
- alpha_blocks: bfloat16 [32, 16, 128, 128], P('alpha'), may hold values from -0.125 to 0.125
- alpha_cols: int32 [32, 16], P('alpha'), may hold values from 0 to 31, all different within a row
- beta_blocks: bfloat16 [32, 16, 128, 128], P('beta'), may hold values from -0.125 to 0.125
- beta_cols: int32 [32, 16], P('beta'), may hold values from 0 to 31, all different within a row
- diagonal: float32 [4096, 4096], P('alpha', 'beta'), may hold values from -1 to 3
Outputs:
- sigma_vectors: bfloat16 [8, 4096, 4096], P(None, 'alpha', 'beta')
Inputs may be any that keep to these rules, and one draw needn't show every extreme that they name: `alpha_cols`: each block-row names 16 different block-columns. `beta_cols`: each block-row names 16 different block-columns.
All inputs are finite; a program needn't handle non-finite values.
Results may differ from a plain program's by a relative error of at most 0.001.
Values may be sent and summed in bfloat16 or wider, within the bound.
A program may use at most 128 MiB of HBM per device.

v0:
```python
import jax
import jax.numpy as jnp
from jax import lax
from jax.sharding import PartitionSpec as P


def alpha_pass(ci_vectors, alpha_blocks, alpha_cols):
    vectors, rows_local, cols_local = ci_vectors.shape
    block = alpha_blocks.shape[-1]
    owned = alpha_blocks.shape[0]
    whole = lax.all_gather(ci_vectors, "alpha", axis=1, tiled=True)
    grid = whole.reshape(vectors, whole.shape[1] // block, block, cols_local)
    picked = grid[:, alpha_cols]
    term = jnp.einsum("rkij,vrkjb->vrib", alpha_blocks, picked, preferred_element_type=jnp.float32)
    return term.reshape(vectors, owned * block, cols_local)


def beta_pass(ci_vectors, beta_blocks, beta_cols):
    vectors, rows_local, cols_local = ci_vectors.shape
    block = beta_blocks.shape[-1]
    turned = lax.all_to_all(ci_vectors, "beta", split_axis=1, concat_axis=2, tiled=True)
    few_rows = turned.shape[1]
    all_cols = turned.shape[2]
    grid = turned.reshape(vectors, few_rows, all_cols // block, block)
    hb_piece = lax.all_gather(beta_blocks, "beta", axis=0, tiled=True)
    col_piece = lax.all_gather(beta_cols.astype(jnp.bfloat16), "beta", axis=0, tiled=True)
    columns = col_piece.astype(jnp.int32)
    count = hb_piece.shape[0]
    picked = grid[:, :, columns]
    term = jnp.einsum("vtnkj,nkij->vtni", picked, hb_piece, preferred_element_type=jnp.float32)
    updated = term.reshape(vectors, few_rows, count * block)
    return lax.all_to_all(updated, "beta", split_axis=2, concat_axis=1, tiled=True)


def shards(ci_vectors, alpha_blocks, alpha_cols, beta_blocks, beta_cols, diagonal):
    alpha_part = alpha_pass(ci_vectors, alpha_blocks, alpha_cols)
    beta_part = beta_pass(ci_vectors, beta_blocks, beta_cols)
    total = alpha_part + beta_part + diagonal[None, :, :] * ci_vectors.astype(jnp.float32)
    return total.astype(jnp.bfloat16)


def solution(mesh):
    placed = (
        P(None, "alpha", "beta"),
        P("alpha", None, None, None),
        P("alpha", None),
        P("beta", None, None, None),
        P("beta", None),
        P("alpha", "beta"),
    )
    return jax.shard_map(
        shards, mesh=mesh, in_specs=placed, out_specs=P(None, "alpha", "beta"), check_vma=False
    )
```

profile of v0, /device:TPU:1, one launch (start us, length us, event | category | flops | bytes accessed | tf_op | source)
XLA Modules:
  0.0 348.9 jit_solution(12847920623883171120)
XLA Ops:
  6.5 0.0 copy-start
  6.5 0.0 all-gather.6.cloned.1.call-start
  6.5 0.7 all-gather.6.cloned.1.call-update
  7.3 0.0 all-gather.4.cloned.1.call-start
  7.3 0.7 all-gather.4.cloned.1.call-update
  8.0 2.9 copy.22
  10.9 12.6 %all-to-all-start = ((bf16[8,512,128]{2,0,1:T(8,128)(2,1)}), bf16[8,512,128]{2,0,1:T(8,128)(2,1)}, u32[]{:S(2)}, u32[]{:S(2)}) async-start(bf16[8,512,128]{2,0,1:T(8,128)(2,1)} %copy.22), calls=%async_computation | async-start | bytes 2097152 | tf_op jit(solution)/shard_map/all_to_all | solution.py:21
  23.5 0.7 convert_bitcast_fusion
  24.2 72.8 %all-gather = bf16[32,1,16]{2,1,0:T(2,128)(2,1)S(1)} all-gather(bf16[1,1,16]{2,1,0:T(2,128)(2,1)S(1)} %convert_bitcast_fusion), channel_id=1, replica_groups=mesh['alpha'=8,'beta'=32] {'beta'}, dimensions={0}, use_global_device_ids=true | all-gather | bytes 1056 | tf_op jit(solution)/shard_map/all_gather | solution.py:26
  97.0 0.1 reshape.25
  97.1 0.0 all-to-all-done
  97.1 1.4 copy.23
  98.4 15.0 %gather_fusion.1 = bf16[512,8,16,128]{3,2,1,0:T(8,128)(2,1)} fusion(bf16[8,16,32,128]{3,1,2,0:T(8,128)(2,1)S(1)} %bitcast.62, s32[1024]{0:T(1024)S(1)} %pad_clamp_fusion), kind=kCustom, calls=%fused_computation.1 | custom fusion | bytes 33556480 | tf_op jit(solution)/shard_map/gather | solution.py:29
  113.4 24.0 %all-gather.6.cloned.1.call-done = bf16[32,16,128,128]{3,2,1,0:T(8,128)(2,1)} async-done(((bf16[1,16,128,128]{3,2,1,0:T(8,128)(2,1)}), bf16[32,16,128,128]{3,2,1,0:T(8,128)(2,1)}) %all-gather.6.cloned.1.call-update) | async-done | bytes 16777232 | tf_op jit(solution)/shard_map/all_gather | solution.py:25
  137.3 14.3 %fusion.9 = f32[8,16,32,128]{3,1,0,2:T(8,128)} fusion(bf16[8,16,32,16,128]{4,1,0,3,2:T(8,128)(2,1)} %bitcast.66, bf16[32,16,128,128]{3,2,1,0:T(8,128)(2,1)} %all-gather.6.cloned.1.call-done), kind=kOutput, calls=%fused_computation.10 | convolution fusion | flops 2147483648 | bytes 35651584 | tf_op jit(solution)/shard_map/vtnkj,nkij->vtni/dot_general | solution.py:30
  151.6 9.5 %copy.33 = f32[8,16,32,128]{1,0,3,2:T(8,128)} copy(f32[8,16,32,128]{3,1,0,2:T(8,128)} %fusion.9) | data formatting | bytes 4194304 | tf_op jit(solution)/shard_map/reshape | solution.py:31
  161.1 13.2 %reshape.42 = f32[32,1,16384]{2,1,0:T(1,128)} reshape(f32[4096,8,16]{2,1,0:T(8,128)} %bitcast.64) | data formatting | bytes 4194304
  174.3 20.3 %all-to-all-start.1 = ((f32[32,1,16384]{2,1,0:T(1,128)}), f32[32,1,16384]{2,1,0:T(1,128)}, u32[]{:S(2)}, u32[]{:S(2)}) async-start(f32[32,1,16384]{2,1,0:T(1,128)} %reshape.42), calls=%async_computation.1 | async-start | bytes 4194304 | tf_op jit(solution)/shard_map/all_to_all | solution.py:32
  194.6 0.0 copy-done.3
  194.7 0.1 reshape.17
  194.8 95.1 %all-gather.4.cloned.1.call-done = bf16[8,4096,128]{2,1,0:T(8,128)(2,1)} async-done(((bf16[8,512,128]{2,1,0:T(8,128)(2,1)}), bf16[8,4096,128]{2,1,0:T(8,128)(2,1)}) %all-gather.4.cloned.1.call-update) | async-done | bytes 8388624 | tf_op jit(solution)/shard_map/all_gather | solution.py:11
  289.9 11.0 %gather_fusion = bf16[64,8,128,128]{3,2,1,0:T(8,128)(2,1)} fusion(bf16[8,32,128,128]{3,2,1,0:T(8,128)(2,1)} %bitcast.67, s32[1024]{0:T(1024)S(1)} %pad_clamp_fusion.1), kind=kCustom, calls=%fused_computation | custom fusion | bytes 33554688 | tf_op jit(solution)/shard_map/gather | solution.py:13
  300.9 0.0 copy-done
  300.9 7.1 %fusion.6 = f32[8,4,128,128]{3,2,0,1:T(8,128)S(1)} fusion(bf16[8,4,16,128,128]{4,3,0,2,1:T(8,128)(2,1)} %bitcast.63, bf16[4,16,128,128]{3,2,1,0:T(8,128)(2,1)S(1)} %copy-done), kind=kOutput, calls=%fused_computation.9 | convolution fusion | flops 2147483648 | bytes 20971520 | tf_op jit(solution)/shard_map/rkij,vrkjb->vrib/dot_general | solution.py:14
  308.0 1.5 copy.21
  309.4 0.0 all-to-all-done.1
  309.4 0.5 broadcast.9
  309.9 8.7 %reduce = f32[32,16384]{1,0:T(8,128)} reduce(f32[32,1,16384]{2,1,0:T(1,128)} %all-to-all-done.1, f32[]{:T(128)} %broadcast.9), dimensions={1}, to_apply=%all_to_all.27.reduce_sub_computation | reduce | bytes 4194308 | tf_op jit(solution)/shard_map/all_to_all | solution.py:32
  318.7 9.2 %reshape.43 = f32[4096,8,16]{2,1,0:T(8,128)} reshape(f32[32,16384]{1,0:T(8,128)} %reduce) | data formatting | bytes 4194304
  327.8 10.7 %copy.28 = f32[8,32,16,128]{3,2,1,0:T(8,128)} copy(f32[8,32,16,128]{2,0,3,1:T(8,128)} %bitcast.65) | data formatting | bytes 4194304 | tf_op jit(solution)/shard_map/all_to_all | solution.py:32
  338.5 0.0 copy-done.1
  338.5 3.5 %fusion.5 = bf16[8,512,128]{2,1,0:T(8,128)(2,1)} fusion(f32[8,32,16,128]{3,2,1,0:T(8,128)} %copy.28, f32[8,4,128,128]{3,2,1,0:T(8,128)} %copy.21, bf16[8,512,128]{2,1,0:T(8,128)(2,1)S(1)} %copy-done.1, f32[512,128]{1,0:T(8,128)S(1)} %copy-done.2), kind=kLoop, calls=%fused_computation.8 | loop fusion | flops 2621440 | bytes 6553600 | tf_op jit(solution)/shard_map/convert_element_type | solution.py:39
  (9 shorter events, 0.0 us)
Async XLA Ops:
  6.5 294.4 %copy-start = (bf16[4,16,128,128]{3,2,1,0:T(8,128)(2,1)S(1)}, bf16[4,16,128,128]{3,2,1,0:T(8,128)(2,1)}, u32[]{:S(2)}) copy-start(bf16[4,16,128,128]{3,2,1,0:T(8,128)(2,1)} %param.7) | copy-start | bytes 6291460
  6.5 130.8 %all-gather.6.cloned.1.call-start = ((), (), s32[]{:S(2)}) async-start(), calls=%async_computation.3 | async-start | bytes 17301504 | tf_op jit(solution)/shard_map/all_gather | solution.py:25
  7.3 282.6 %all-gather.4.cloned.1.call-start = ((), (), s32[]{:S(2)}) async-start(), calls=%async_computation.2 | async-start | bytes 9437184 | tf_op jit(solution)/shard_map/all_gather | solution.py:11
  10.9 86.2 %all-to-all-start = ((bf16[8,512,128]{2,0,1:T(8,128)(2,1)}), bf16[8,512,128]{2,0,1:T(8,128)(2,1)}, u32[]{:S(2)}, u32[]{:S(2)}) async-start(bf16[8,512,128]{2,0,1:T(8,128)(2,1)} %copy.22), calls=%async_computation | async-start | bytes 2097152 | tf_op jit(solution)/shard_map/all_to_all | solution.py:21
  161.1 33.5 %copy-start.3 = (s32[4,16]{1,0:T(4,128)S(1)}, s32[4,16]{1,0:T(4,128)}, u32[]{:S(2)}) copy-start(s32[4,16]{1,0:T(4,128)} %param.8) | copy-start | bytes 772
  174.3 135.1 %all-to-all-start.1 = ((f32[32,1,16384]{2,1,0:T(1,128)}), f32[32,1,16384]{2,1,0:T(1,128)}, u32[]{:S(2)}, u32[]{:S(2)}) async-start(f32[32,1,16384]{2,1,0:T(1,128)} %reshape.42), calls=%async_computation.1 | async-start | bytes 4194304 | tf_op jit(solution)/shard_map/all_to_all | solution.py:32
  327.8 10.7 %copy-start.1 = (bf16[8,512,128]{2,1,0:T(8,128)(2,1)S(1)}, bf16[8,512,128]{2,1,0:T(8,128)(2,1)}, u32[]{:S(2)}) copy-start(bf16[8,512,128]{2,1,0:T(8,128)(2,1)} %param.6) | copy-start | bytes 3145732
  327.8 10.7 %copy-start.2 = (f32[512,128]{1,0:T(8,128)S(1)}, f32[512,128]{1,0:T(8,128)}, u32[]{:S(2)}) copy-start(f32[512,128]{1,0:T(8,128)} %param.11) | copy-start | bytes 786436
Sparse Core Ops, SparseCore 0:
  9.9 127.4 all-gather.5
  139.1 150.6 all-gather.3
where the time goes:
time: 350 us; the launch traced here: 349 us
  waiting for transfers between devices  120 us (34%)
  local copies, waits for them, and re-layouts  74.9 us (21%)
  blocking collectives  72.8 us (21%)
  starting transfers between devices  33 us (9%)
  matrix products  21.3 us (6%)
  between operations  13.5 us (4%)
  other arithmetic  13 us (4%)
    all_gather x1, waiting for transfers between devices, alpha_pass(): whole = lax.all_gather(ci_vectors, 'alpha', axis=1, tiled=True)  95.1 us
    all_gather x1, blocking collectives, beta_pass(): lax.all_gather(beta_cols.astype(jnp.bfloat16), 'beta', axis=0, tiled=True)  72.8 us
    unnamed x11, local copies, waits for them, and re-layouts  25.2 us
    all_gather x1, waiting for transfers between devices, beta_pass(): hb_piece = lax.all_gather(beta_blocks, 'beta', axis=0, tiled=True)  24 us
    all_to_all x1, starting transfers between devices, beta_pass(): lax.all_to_all(updated, 'beta', split_axis=2, concat_axis=1, tiled=True)  20.3 us
    gather x1, local copies, waits for them, and re-layouts, beta_pass(): picked = grid[:, :, columns]  15 us
    dot_general x1, matrix products, beta_pass(): jnp.einsum('vtnkj,nkij->vtni', picked, hb_piece, preferred_element_type=j...  14.3 us
    all_to_all x1, starting transfers between devices, beta_pass(): lax.all_to_all(ci_vectors, 'beta', split_axis=1, concat_axis=2, tiled=True)  12.6 us
  transfers between devices with their start and end apart: 4, of which 2 were waited for; matrix products, arithmetic and copies ran while one was open for 22% of the time, Pallas kernels for 0%

commit v1 on v0

--- a/solution.py
+++ b/solution.py
@@ -22,7 +22,17 @@
     few_rows = turned.shape[1]
     all_cols = turned.shape[2]
     grid = turned.reshape(vectors, few_rows, all_cols // block, block)
-    hb_piece = lax.all_gather(beta_blocks, "beta", axis=0, tiled=True)
+
+    def attach_spots_for(my_tile):
+        pages = []
+        for _ in range(lax.axis_size("beta")):
+            pages.append(my_tile)
+        value_now = jnp.concatenate(
+            lax.all_to_all(jnp.stack(pages, axis=0), "beta", split_axis=0, concat_axis=0), 0
+        )
+        return value_now
+
+    hb_piece = attach_spots_for(beta_blocks)
     col_piece = lax.all_gather(beta_cols.astype(jnp.bfloat16), "beta", axis=0, tiled=True)
     columns = col_piece.astype(jnp.int32)
     count = hb_piece.shape[0]

time: 350 us -> 688 us (1.97); the launches traced: 349 us -> 676 us
  blocking collectives: 72.8 us -> 516 us
  waiting for transfers between devices: 120 us -> 20.6 us
  starting transfers between devices: 33 us -> 11.6 us
    all_gather x1, blocking collectives: 72.8 us -> 476 us  [beta_pass(): lax.all_gather(beta_cols.astype(jnp.bfloat16), 'beta', axis=0, tiled=True)]
    all_gather x1, waiting for transfers between devices: 95.1 us -> 0.01 us  [alpha_pass(): whole = lax.all_gather(ci_vectors, 'alpha', axis=1, tiled=True)]
    all_to_all x0 -> x1, blocking collectives: none -> 40.1 us  [beta_pass(): lax.all_to_all(ci_vectors, 'beta', split_axis=1, concat_axis=2, tiled=True)]
    all_gather x1 -> x0, waiting for transfers between devices: 24 us -> none  [beta_pass(): hb_piece = lax.all_gather(beta_blocks, 'beta', axis=0, tiled=True)]
    all_to_all x1, waiting for transfers between devices: 0.01 us -> 19.9 us  [beta_pass(): lax.all_to_all(updated, 'beta', split_axis=2, concat_axis=1, tiled=True)]
    all_to_all x1, starting transfers between devices: 20.3 us -> 4.9 us  [beta_pass(): lax.all_to_all(updated, 'beta', split_axis=2, concat_axis=1, tiled=True)]
    another operation x0 -> x1, local copies, waits for them, and re-layouts: none -> 7.01 us  [attach_spots_for(): jnp.stack(pages, axis=0)]
    unnamed x11 -> x13, local copies, waits for them, and re-layouts: 25.2 us -> 24.3 us
  transfers between devices with their start and end apart: 4 -> 3, of which waited for: 2 -> 1; matrix products, arithmetic and copies ran while one was open for 22% -> 11% of each run, Pallas kernels for 0% -> 0%
where the time goes in v1:
time: 688 us; the launch traced here: 676 us
  blocking collectives  516 us (75%)
  local copies, waits for them, and re-layouts  81 us (12%)
  matrix products  21.3 us (3%)
  waiting for transfers between devices  20.6 us (3%)
  between operations  13.5 us (2%)
  other arithmetic  12.3 us (2%)
  starting transfers between devices  11.6 us (2%)
    all_gather x1, blocking collectives, beta_pass(): lax.all_gather(beta_cols.astype(jnp.bfloat16), 'beta', axis=0, tiled=True)  476 us
    all_to_all x1, blocking collectives, beta_pass(): lax.all_to_all(ci_vectors, 'beta', split_axis=1, concat_axis=2, tiled=True)  40.1 us
    unnamed x13, local copies, waits for them, and re-layouts  24.3 us
    all_to_all x1, waiting for transfers between devices, beta_pass(): lax.all_to_all(updated, 'beta', split_axis=2, concat_axis=1, tiled=True)  19.9 us
    gather x1, local copies, waits for them, and re-layouts, beta_pass(): picked = grid[:, :, columns]  15 us
    dot_general x1, matrix products, beta_pass(): jnp.einsum('vtnkj,nkij->vtni', picked, hb_piece, preferred_element_type=j...  14.2 us
  transfers between devices with their start and end apart: 3, of which 1 were waited for; matrix products, arithmetic and copies ran while one was open for 11% of the time, Pallas kernels for 0%

profile of v1, /device:TPU:1, one launch (start us, length us, event | category | flops | bytes accessed | tf_op | source)
XLA Modules:
  0.0 676.0 jit_solution(7027852549541332283)
XLA Ops:
  6.5 0.0 copy-start
  6.5 2.1 copy.22
  8.6 40.1 %all_to_all.38 = bf16[8,512,128]{2,0,1:T(8,128)(2,1)} all-to-all(bf16[8,512,128]{2,0,1:T(8,128)(2,1)S(1)} %copy.22), channel_id=1, replica_groups=mesh['alpha'=8,'beta'=32] {'beta'}, dimensions={1} | all-to-all | bytes 2097152 | tf_op jit(solution)/shard_map/all_to_all | solution.py:21
  48.7 7.0 %stack.2 = bf16[32,1,16,128,128]{4,3,2,1,0:T(8,128)(2,1)} broadcast(bf16[16,128,128]{2,1,0:T(8,128)(2,1)} %bitcast.70), dimensions={2,3,4} | broadcast | bytes 17301504 | tf_op jit(solution)/shard_map/stack | solution.py:31
  55.7 6.7 all-to-all-start.1
  62.4 0.0 all-gather.3.cloned.1.call-start
  62.4 0.7 all-gather.3.cloned.1.call-update
  63.1 0.0 copy-done.4
  63.1 475.6 %all-gather = bf16[32,1,16]{2,1,0:T(2,128)(2,1)S(1)} all-gather(bf16[1,1,16]{2,1,0:T(2,128)(2,1)S(1)} %convert_bitcast_fusion), channel_id=1, replica_groups=mesh['alpha'=8,'beta'=32] {'beta'}, dimensions={0}, use_global_device_ids=true | all-gather | bytes 1056 | tf_op jit(solution)/shard_map/all_gather | solution.py:36
  538.8 0.1 reshape.32
  538.9 1.4 copy.23
  540.3 15.0 %gather_fusion.1 = bf16[512,8,16,128]{3,2,1,0:T(8,128)(2,1)} fusion(bf16[8,16,32,128]{3,1,2,0:T(8,128)(2,1)S(1)} %bitcast.64, s32[1024]{0:T(1024)S(1)} %pad_clamp_fusion), kind=kCustom, calls=%fused_computation.1 | custom fusion | bytes 33556480 | tf_op jit(solution)/shard_map/gather | solution.py:39
  555.2 0.0 all-to-all-done.1
  555.2 14.2 %fusion.9 = f32[8,16,32,128]{3,1,0,2:T(8,128)} fusion(bf16[8,16,32,16,128]{4,1,0,3,2:T(8,128)(2,1)} %bitcast.68, bf16[32,1,16,128,128]{4,3,2,1,0:T(8,128)(2,1)} %all-to-all-done.1), kind=kOutput, calls=%fused_computation.10 | convolution fusion | flops 2147483648 | bytes 35651584 | tf_op jit(solution)/shard_map/vtnkj,nkij->vtni/dot_general | solution.py:40
  569.5 9.5 %copy.33 = f32[8,16,32,128]{1,0,3,2:T(8,128)} copy(f32[8,16,32,128]{3,1,0,2:T(8,128)} %fusion.9) | data formatting | bytes 4194304 | tf_op jit(solution)/shard_map/reshape | solution.py:41
  579.0 13.0 %reshape.49 = f32[32,1,16384]{2,1,0:T(1,128)} reshape(f32[4096,8,16]{2,1,0:T(8,128)} %bitcast.66) | data formatting | bytes 4194304
  592.0 4.9 all-to-all-start.2
  596.9 0.0 copy-done.3
  596.9 0.1 reshape.24
  597.0 0.0 all-gather.3.cloned.1.call-done
  597.0 11.0 %gather_fusion = bf16[64,8,128,128]{3,2,1,0:T(8,128)(2,1)} fusion(bf16[8,32,128,128]{3,2,1,0:T(8,128)(2,1)} %bitcast.69, s32[1024]{0:T(1024)S(1)} %pad_clamp_fusion.1), kind=kCustom, calls=%fused_computation | custom fusion | bytes 33554688 | tf_op jit(solution)/shard_map/gather | solution.py:13
  608.0 0.0 copy-done
  608.0 7.0 %fusion.6 = f32[8,4,128,128]{3,2,0,1:T(8,128)S(1)} fusion(bf16[8,4,16,128,128]{4,3,0,2,1:T(8,128)(2,1)} %bitcast.65, bf16[4,16,128,128]{3,2,1,0:T(8,128)(2,1)S(1)} %copy-done), kind=kOutput, calls=%fused_computation.9 | convolution fusion | flops 2147483648 | bytes 20971520 | tf_op jit(solution)/shard_map/rkij,vrkjb->vrib/dot_general | solution.py:14
  615.1 1.5 copy.21
  616.6 19.9 %all-to-all-done.2 = f32[32,1,16384]{2,1,0:T(1,128)} async-done(((f32[32,1,16384]{2,1,0:T(1,128)}), f32[32,1,16384]{2,1,0:T(1,128)}, u32[]{:S(2)}, u32[]{:S(2)}) %all-to-all-start.2) | async-done | bytes 2097184 | tf_op jit(solution)/shard_map/all_to_all | solution.py:42
  636.5 0.5 broadcast.12
  637.0 8.7 %reduce = f32[32,16384]{1,0:T(8,128)} reduce(f32[32,1,16384]{2,1,0:T(1,128)} %all-to-all-done.2, f32[]{:T(128)} %broadcast.12), dimensions={1}, to_apply=%all_to_all.31.reduce_sub_computation | reduce | bytes 4194308 | tf_op jit(solution)/shard_map/all_to_all | solution.py:42
  645.7 9.2 %reshape.50 = f32[4096,8,16]{2,1,0:T(8,128)} reshape(f32[32,16384]{1,0:T(8,128)} %reduce) | data formatting | bytes 4194304
  654.9 10.7 %copy.28 = f32[8,32,16,128]{3,2,1,0:T(8,128)} copy(f32[8,32,16,128]{2,0,3,1:T(8,128)} %bitcast.67) | data formatting | bytes 4194304 | tf_op jit(solution)/shard_map/all_to_all | solution.py:42
  665.6 0.0 copy-done.1
  665.6 0.0 copy-done.2
  665.6 3.5 fusion.5
  (10 shorter events, 0.1 us)
Async XLA Ops:
  6.5 601.5 %copy-start = (bf16[4,16,128,128]{3,2,1,0:T(8,128)(2,1)S(1)}, bf16[4,16,128,128]{3,2,1,0:T(8,128)(2,1)}, u32[]{:S(2)}) copy-start(bf16[4,16,128,128]{3,2,1,0:T(8,128)(2,1)} %param.7) | copy-start | bytes 6291460
  55.7 7.4 %copy-start.4 = (s32[1,16]{1,0:T(1,128)S(1)}, s32[1,16]{1,0:T(1,128)}, u32[]{:S(2)}) copy-start(s32[1,16]{1,0:T(1,128)} %param.10) | copy-start | bytes 196
  55.7 499.5 %all-to-all-start.1 = ((bf16[32,1,16,128,128]{4,3,2,1,0:T(8,128)(2,1)}), bf16[32,1,16,128,128]{4,3,2,1,0:T(8,128)(2,1)}, u32[]{:S(2)}, u32[]{:S(2)}) async-start(bf16[32,1,16,128,128]{4,3,2,1,0:T(8,128)(2,1)} %stack.2), calls=%async_computation.1 | async-start | bytes 33554432 | tf_op jit(solution)/shard_map/all_to_all | solution.py:31
  62.4 534.6 %all-gather.3.cloned.1.call-start = ((), (), s32[]{:S(2)}) async-start(), calls=%async_computation.3 | async-start | bytes 9437184 | tf_op jit(solution)/shard_map/all_gather | solution.py:11
  579.0 17.9 %copy-start.3 = (s32[4,16]{1,0:T(4,128)S(1)}, s32[4,16]{1,0:T(4,128)}, u32[]{:S(2)}) copy-start(s32[4,16]{1,0:T(4,128)} %param.8) | copy-start | bytes 772
  592.0 44.5 %all-to-all-start.2 = ((f32[32,1,16384]{2,1,0:T(1,128)}), f32[32,1,16384]{2,1,0:T(1,128)}, u32[]{:S(2)}, u32[]{:S(2)}) async-start(f32[32,1,16384]{2,1,0:T(1,128)} %reshape.49), calls=%async_computation.2 | async-start | bytes 4194304 | tf_op jit(solution)/shard_map/all_to_all | solution.py:42
  654.9 10.7 %copy-start.1 = (bf16[8,512,128]{2,1,0:T(8,128)(2,1)S(1)}, bf16[8,512,128]{2,1,0:T(8,128)(2,1)}, u32[]{:S(2)}) copy-start(bf16[8,512,128]{2,1,0:T(8,128)(2,1)} %param.6) | copy-start | bytes 3145732
  654.9 10.7 %copy-start.2 = (f32[512,128]{1,0:T(8,128)S(1)}, f32[512,128]{1,0:T(8,128)}, u32[]{:S(2)}) copy-start(f32[512,128]{1,0:T(8,128)} %param.11) | copy-start | bytes 786436
Sparse Core Ops, SparseCore 0:
  65.0 298.8 all-gather.2
